TPU v7x, 128 devices: a whole 4x4x4 slice. The times are simulated.
128 devices in a mesh: ctx: 32 (over x, z, y_lo), tp: 4 (over y_hi, core).
Axes of the slice: x: 4, y: 4 (y_hi: 2, y_lo: 2; y = y_hi * 2 + y_lo), z: 4, core: 2. Of those that a mesh axis runs over, the one named last changes fastest.
Arguments:
- queries: bfloat16 [1024, 8192], P('ctx', 'tp'), may hold values from -15 to 15
- new_keys: bfloat16 [1024, 1024], P('ctx', 'tp'), may hold values from -6 to 6
- new_values: bfloat16 [1024, 1024], P('ctx', 'tp'), may hold values from -6 to 6
- cache_keys: bfloat16 [131072, 1024], P('ctx', 'tp'), may hold values from -6 to 6
- cache_values: bfloat16 [131072, 1024], P('ctx', 'tp'), may hold values from -6 to 6
- keep_tiles: int32 [32, 8, 24], P('ctx', 'tp'), may hold values from 0 to 31, as said below
- tile_count: int32 [32, 8], P('ctx', 'tp'), may hold values from 1 to 24
- owner_slot: int32 [32], replicated, may hold values from 0 to 31, each once
- out_weight: bfloat16 [8192, 8192], P('tp', 'ctx'), may hold values from -0.0625 to 0.0625
Outputs:
- projected_out: float32 [1024, 8192], P('tp', 'ctx')
Inputs may be any that keep to these rules, and one draw needn't show every extreme that they name: `keep_tiles`: the 24 entries of each keep list are distinct tile numbers; entries at or past tile_count are ignored.
All inputs are finite; a program needn't handle non-finite values.
Results may differ from a plain program's by a relative error of at most 0.0055.
Values may be sent and summed in bfloat16 or wider, within the bound.
A program may use at most 128 MiB of HBM per device.

v0:
```python
import jax
import jax.numpy as jnp
from jax import lax
from jax.sharding import PartitionSpec as P

DH = 128
TILE = 128
TB = 4
NEG_INF = -jnp.inf


def fold_scores(state_now, scores, value_rows):
    run_max, run_total, run_sum = state_now
    new_max = jnp.maximum(run_max, jnp.max(scores, axis=-1))
    shrink = jnp.exp(run_max - new_max)
    weights = jnp.exp(scores - new_max[..., None])
    run_total = run_total * shrink + jnp.sum(weights, axis=-1)
    mixture = jnp.einsum(
        "rhk,kd->rhd", weights.astype(jnp.bfloat16), value_rows, preferred_element_type=jnp.float32
    )
    run_sum = run_sum * shrink[..., None] + mixture
    return (new_max, run_total, run_sum)


def body(
    queries,
    new_keys,
    new_values,
    cache_keys,
    cache_values,
    keep_tiles,
    tile_count,
    owner_slot,
    out_weight,
):
    q_dev = queries.shape[0]
    kv_local = new_keys.shape[1] // DH
    q_local = queries.shape[1] // DH
    group_size = q_local // kv_local
    ctx_count = lax.axis_size("ctx")
    total_rows = q_dev * ctx_count
    my_index = lax.axis_index("ctx")
    score_scale = DH ** (-0.5)
    slot_count = keep_tiles.shape[2]
    key_place = owner_slot[my_index] * q_dev + jnp.arange(q_dev, dtype=jnp.int32)
    tiled_keys = cache_keys.reshape(-1, TILE, kv_local, DH)
    tiled_values = cache_values.reshape(-1, TILE, kv_local, DH)
    kept_keys = [
        jnp.take(tiled_keys[:, :, kv_head, :], keep_tiles[0, kv_head], axis=0)
        for kv_head in range(kv_local)
    ]
    kept_values = [
        jnp.take(tiled_values[:, :, kv_head, :], keep_tiles[0, kv_head], axis=0)
        for kv_head in range(kv_local)
    ]
    query_rows = lax.all_gather(queries, "ctx", axis=0, tiled=True)
    row_count = query_rows.shape[0]
    row_ids = jnp.arange(row_count, dtype=jnp.int32)
    query_place = owner_slot[row_ids // q_dev] * q_dev + row_ids % q_dev
    causal = query_place[:, None] >= key_place[None, :]
    pieces_max = []
    pieces_total = []
    pieces_sum = []
    for kv_head in range(kv_local):
        query_head = query_rows[
            :, kv_head * group_size * DH : (kv_head + 1) * group_size * DH
        ].reshape(row_count, group_size, DH)
        start_state = (
            jnp.full((row_count, group_size), NEG_INF, jnp.float32),
            jnp.zeros((row_count, group_size), jnp.float32),
            jnp.zeros((row_count, group_size, DH), jnp.float32),
        )
        live_count = tile_count[0, kv_head]

        def tile_block(
            block_id, state_inner, kv_head=kv_head, query_head=query_head, live_count=live_count
        ):
            key_block = lax.dynamic_slice_in_dim(kept_keys[kv_head], block_id * TB, TB, 0).reshape(
                TB * TILE, DH
            )
            value_block = lax.dynamic_slice_in_dim(
                kept_values[kv_head], block_id * TB, TB, 0
            ).reshape(TB * TILE, DH)
            tile_ids = block_id * TB + jnp.arange(TB, dtype=jnp.int32)
            live_keys = jnp.repeat(tile_ids < live_count, TILE)
            scores = (
                jnp.einsum("rhd,kd->rhk", query_head, key_block, preferred_element_type=jnp.float32)
                * score_scale
            )
            scores = jnp.where(live_keys[None, None, :], scores, NEG_INF)
            return fold_scores(state_inner, scores, value_block)

        block_limit = slot_count // TB
        state_head = lax.fori_loop(0, block_limit, tile_block, start_state)
        fresh_keys = new_keys[:, kv_head * DH : (kv_head + 1) * DH]
        fresh_values = new_values[:, kv_head * DH : (kv_head + 1) * DH]
        scores = (
            jnp.einsum("rhd,kd->rhk", query_head, fresh_keys, preferred_element_type=jnp.float32)
            * score_scale
        )
        scores = jnp.where(causal[:, None, :], scores, NEG_INF)
        head_max, head_total, head_sum = fold_scores(state_head, scores, fresh_values)
        pieces_max.append(head_max)
        pieces_total.append(head_total)
        pieces_sum.append(head_sum.reshape(row_count, group_size * DH))
    maxima_all = jnp.concatenate(pieces_max, axis=1)
    totals_all = jnp.concatenate(pieces_total, axis=1)
    sums_all = jnp.concatenate(pieces_sum, axis=1)
    top_max = lax.pmax(maxima_all, "ctx")
    factor = jnp.exp(maxima_all - top_max)
    scaled = (sums_all.reshape(total_rows, q_local, DH) * factor[..., None]).reshape(
        total_rows, q_local * DH
    )
    numerator, denominator = (
        lax.psum_scatter(scaled, "ctx", scatter_dimension=0, tiled=True),
        lax.psum_scatter(totals_all * factor, "ctx", scatter_dimension=0, tiled=True),
    )
    attn_rows = (
        (numerator.reshape(q_dev, q_local, DH) / denominator[..., None])
        .reshape(q_dev, q_local * DH)
        .astype(jnp.bfloat16)
    )
    projected = jnp.dot(
        lax.all_gather(attn_rows, "ctx", axis=0, tiled=True),
        out_weight,
        preferred_element_type=jnp.float32,
    )
    return lax.psum_scatter(projected, "tp", scatter_dimension=0, tiled=True)


def solution(mesh):
    return jax.shard_map(
        body,
        mesh=mesh,
        in_specs=(
            P("ctx", "tp"),
            P("ctx", "tp"),
            P("ctx", "tp"),
            P("ctx", "tp"),
            P("ctx", "tp"),
            P("ctx", "tp", None),
            P("ctx", "tp"),
            P(),
            P("tp", "ctx"),
        ),
        out_specs=P("tp", "ctx"),
        check_vma=False,
    )
```

profile of v0, /device:TPU:1, one launch (start us, length us, event | category | flops | bytes accessed | tf_op | source)
XLA Modules:
  0.0 1224.2 jit_solution(18363022142407999071)
XLA Ops:
  14.0 6.1 fusion.48
  43.7 15.2 %fusion.43 = s32[1024]{0:T(1024)S(1)} fusion(pred[1024]{0:T(1024)(128)(4,1)S(1)} %compare_reduce_fusion, pred[1024]{0:T(1024)(128)(4,1)S(1)} %compare_reduce_fusion.1, pred[1024]{0:T(1024)(128)(4,1)S(1)} %compare_reduce_fusion.2, pred[1024]{0:T(1024)(128)(4,1)S(1)} %compare_reduce_fusion.3, pred[1024]{0:T(1024)(128)(4,1)S(1)} %compare_reduce_fusion.4, ...), kind=kLoop, calls=%fused_computation.122 | loop fusion | flops 33792 | bytes 33892 | tf_op jit(solution)/shard_map/add | solution.py:59
  64.2 85.2 %all-gather.3.cloned.1.call-done = bf16[1024,2048]{1,0:T(8,128)(2,1)} async-done(((bf16[32,2048]{1,0:T(8,128)(2,1)}), bf16[1024,2048]{1,0:T(8,128)(2,1)}) %all-gather.3.cloned.1.call-update) | async-done | bytes 4194320 | tf_op jit(solution)/shard_map/all_gather | solution.py:56
  172.9 103.2 %while.37 = (s32[]{:T(128)}, f32[1024,8]{0,1:T(8,128)S(1)}, f32[1024,8]{0,1:T(8,128)S(1)}, f32[1024,8,128]{2,0,1:T(8,128)}, s32[]{:T(128)}, /*index=5*/bf16[24,1...) while((s32[]{:T(128)}, f32[1024,8]{0,1:T(8,128)S(1)}, ...), condition=%wide.region_8.10_spmd.clone, body=%wide.region_5.9_spmd.clone.sunk | while | flops 2196807680 | bytes 62130376 | solution.py:94
  182.4 6.3 fusion.93
  198.3 7.9 fusion.93
  215.8 7.9 fusion.93
  233.3 7.9 fusion.93
  250.7 7.9 fusion.93
  268.2 7.9 fusion.93
  281.4 93.2 %while.36 = (s32[]{:T(128)}, f32[1024,8]{0,1:T(8,128)S(1)}, f32[1024,8]{0,1:T(8,128)S(1)}, f32[1024,8,128]{2,0,1:T(8,128)}, s32[]{:T(128)}, /*index=5*/bf16[24,1...) while((s32[]{:T(128)}, f32[1024,8]{0,1:T(8,128)S(1)}, ...), condition=%wide.region_3.5_spmd.clone, body=%wide.region_0.4_spmd.clone.sunk | while | flops 2196807680 | bytes 62130376 | solution.py:94
  289.3 6.3 fusion.86
  303.6 7.9 fusion.86
  319.4 7.9 fusion.86
  335.2 7.9 fusion.86
  350.9 7.9 fusion.86
  366.7 7.9 fusion.86
  389.6 269.2 %all-reduce.2.cloned.1.call-done = f32[1024,16]{0,1:T(8,128)} async-done(((f32[1024,16]{0,1:T(8,128)}), f32[1024,16]{0,1:T(8,128)}) %all-reduce.2.cloned.1.call-update) | async-done | bytes 65552 | tf_op jit(solution)/shard_map/pmax | solution.py:109
  660.8 8.7 maximum_multiply_fusion
  669.4 9.1 copy.61
  678.7 130.2 %reduce-scatter.12.cloned.1.call-done = f32[32,16]{1,0:T(8,128)} async-done(((f32[1024,16]{1,0:T(8,128)}), f32[32,16]{1,0:T(8,128)}) %reduce-scatter.12.cloned.1.call-update) | async-done | bytes 2064
  809.7 209.7 %reduce-scatter.10.cloned.1.call-done = f32[32,2048]{1,0:T(8,128)} async-done(((f32[1024,2048]{1,0:T(8,128)}), f32[32,2048]{1,0:T(8,128)}) %reduce-scatter.10.cloned.1.call-update) | async-done | bytes 262160
  1021.7 138.5 %all-gather.5.cloned.1.call-done = bf16[1024,2048]{1,0:T(8,128)(2,1)} async-done(((bf16[32,2048]{1,0:T(8,128)(2,1)}), bf16[1024,2048]{1,0:T(8,128)(2,1)}) %all-gather.5.cloned.1.call-update) | async-done | bytes 4194320 | tf_op jit(solution)/shard_map/all_gather | solution.py:124
  1164.6 52.8 %reduce-scatter.8.cloned.1.call-done = f32[256,256]{1,0:T(8,128)} async-done(((f32[1024,256]{1,0:T(8,128)}), f32[256,256]{1,0:T(8,128)}) %reduce-scatter.8.cloned.1.call-update) | async-done | bytes 262160 | tf_op jit(solution)/shard_map/reduce_scatter | solution.py:128
  (211 shorter events, 193.3 us)
Async XLA Ops:
  6.5 1153.6 %copy-start = (bf16[2048,256]{1,0:T(8,128)(2,1)S(1)}, bf16[2048,256]{1,0:T(8,128)(2,1)}, u32[]{:S(2)}) copy-start(bf16[2048,256]{1,0:T(8,128)(2,1)} %param.23) | copy-start | bytes 3145732
  6.5 142.9 %all-gather.3.cloned.1.call-start = ((), (), s32[]{:S(2)}) async-start(), calls=%async_computation.3 | async-start | bytes 4325376 | tf_op jit(solution)/shard_map/all_gather | solution.py:56
  7.3 651.6 %all-reduce.2.cloned.1.call-start = ((), (), s32[]{:S(2)}) async-start(), calls=%async_computation.4 | async-start | bytes 131072 | tf_op jit(solution)/shard_map/pmax | solution.py:109
  7.4 6.6 copy-start.13
  28.5 4.2 copy-start.5
  28.5 7.3 copy-start.7
  28.5 14.5 %copy-start.12 = (s32[1,2]{1,0:T(1,128)S(1)}, s32[1,2]{1,0:T(1,128)}, u32[]{:S(2)}) copy-start(s32[1,2]{1,0:T(1,128)} %param.21) | copy-start | bytes 28
  34.3 27.5 %copy-start.6 = (bf16[24,128,128]{2,1,0:T(8,128)(2,1)S(1)}, bf16[24,128,128]{2,1,0:T(8,128)(2,1)}, u32[]{:S(2)}) copy-start(bf16[24,128,128]{2,1,0:T(8,128)(2,1)} %gather_fusion.1) | copy-start | bytes 2359300
  156.1 7.0 copy-start.10
  163.1 3.9 copy-start.1
  374.6 5.5 copy-start.9
  374.6 5.5 copy-start.4
  374.6 5.8 copy-start.8
  374.6 6.4 copy-start.3
  374.6 6.7 copy-start.11
  381.3 427.6 %reduce-scatter.12.cloned.1.call-start = ((), (), s32[]{:S(2)}) async-start(), calls=%async_computation.8 | async-start | bytes 540672
  381.4 5.5 copy-start.2
  660.7 358.6 %reduce-scatter.10.cloned.1.call-start = ((), (), s32[]{:S(2)}) async-start(), calls=%async_computation.7 | async-start | bytes 8650752
  678.6 481.6 %all-gather.5.cloned.1.call-start = ((), (), s32[]{:S(2)}) async-start(), calls=%async_computation.5 | async-start | bytes 4325376 | tf_op jit(solution)/shard_map/all_gather | solution.py:124
  1021.6 195.8 %reduce-scatter.8.cloned.1.call-start = ((), (), s32[]{:S(2)}) async-start(), calls=%async_computation.6 | async-start | bytes 1310720 | tf_op jit(solution)/shard_map/reduce_scatter | solution.py:128
Sparse Core Ops, SparseCore 0:
  9.0 140.3 all-gather.2
  381.4 277.4 all-reduce.1
  661.3 147.4 reduce-scatter.11
  811.1 208.1 reduce-scatter.9
  1021.7 138.3 all-gather.4
  1164.7 52.6 reduce-scatter.7
where the time goes:
time: 1230 us; the launch traced here: 1220 us
  waiting for transfers between devices  886 us (72%)
  matrix products  148 us (12%)
  other arithmetic  90.1 us (7%)
  local copies, waits for them, and re-layouts  84.6 us (7%)
  between operations  14.4 us (1%)
    unnamed x8, waiting for transfers between devices  341 us
    pmax x1, waiting for transfers between devices, body(): top_max = lax.pmax(maxima_all, 'ctx')  269 us
    all_gather x1, waiting for transfers between devices, body(): lax.all_gather(attn_rows, 'ctx', axis=0, tiled=True)  139 us
    dot_general x14, matrix products, fold_scores(): jnp.einsum('rhk,kd->rhd', weights.astype(jnp.bfloat16), value_rows, prefe...  99.5 us
    all_gather x1, waiting for transfers between devices, body(): query_rows = lax.all_gather(queries, 'ctx', axis=0, tiled=True)  85.2 us
    reduce_scatter x1, waiting for transfers between devices, body(): return lax.psum_scatter(projected, 'tp', scatter_dimension=0, tiled=True)  52.8 us
    reduce_sum x14, other arithmetic, fold_scores(): run_total = run_total * shrink + jnp.sum(weights, axis=-1)  45.9 us
    dot_general x12, matrix products, tile_block(): jnp.einsum('rhd,kd->rhk', query_head, key_block, preferred_element_type=j...  38.1 us
  transfers between devices with their start and end apart: 6, of which 6 were waited for; matrix products, arithmetic and copies ran while one was open for 7% of the time, Pallas kernels for 0%

commit v1 on v0

--- a/solution.py
+++ b/solution.py
@@ -121,7 +121,9 @@
         .astype(jnp.bfloat16)
     )
     projected = jnp.dot(
-        lax.all_gather(attn_rows, "ctx", axis=0, tiled=True),
+        jnp.concatenate(
+            lax.all_to_all(jnp.stack([attn_rows] * lax.axis_size("ctx")), "ctx", 0, 0), axis=0
+        ),
         out_weight,
         preferred_element_type=jnp.float32,
     )

time: 1230 us -> 1120 us (0.911)
  waiting for transfers between devices: 886 us -> 727 us
  blocking collectives: 0 us -> 56.6 us
    all_gather x1 -> x0, waiting for transfers between devices: 139 us -> none  [body(): lax.all_gather(attn_rows, 'ctx', axis=0, tiled=True)]
    all_to_all x0 -> x1, blocking collectives: none -> 56.6 us  [body(): lax.all_to_all(jnp.stack([attn_rows] * lax.axis_size('ctx')), 'ctx', 0, 0)]
    reduce_scatter x1, waiting for transfers between devices: 52.8 us -> 31.7 us  [body(): return lax.psum_scatter(projected, 'tp', scatter_dimension=0, tiled=True)]
    unnamed x8 -> x7, waiting for transfers between devices: 341 us -> 341 us
  transfers between devices with their start and end apart: 6 -> 5, of which waited for: 6 -> 5; matrix products, arithmetic and copies ran while one was open for 7% -> 7% of each run, Pallas kernels for 0% -> 0%
where the time goes in v1:
time: 1120 us
  waiting for transfers between devices  727 us (65%)
  matrix products  146 us (13%)
  other arithmetic  90.1 us (8%)
  local copies, waits for them, and re-layouts  84.5 us (8%)
  blocking collectives  56.6 us (5%)
  between operations  14.1 us (1%)
    unnamed x7, waiting for transfers between devices  341 us
    pmax x1, waiting for transfers between devices, body(): top_max = lax.pmax(maxima_all, 'ctx')  269 us
    dot_general x14, matrix products, fold_scores(): jnp.einsum('rhk,kd->rhd', weights.astype(jnp.bfloat16), value_rows, prefe...  99.5 us
    all_gather x1, waiting for transfers between devices, body(): query_rows = lax.all_gather(queries, 'ctx', axis=0, tiled=True)  85.2 us
    all_to_all x1, blocking collectives, body(): lax.all_to_all(jnp.stack([attn_rows] * lax.axis_size('ctx')), 'ctx', 0, 0)  56.6 us
    reduce_sum x14, other arithmetic, fold_scores(): run_total = run_total * shrink + jnp.sum(weights, axis=-1)  45.9 us
    dot_general x12, matrix products, tile_block(): jnp.einsum('rhd,kd->rhk', query_head, key_block, preferred_element_type=j...  38.1 us
    reduce_scatter x1, waiting for transfers between devices, body(): return lax.psum_scatter(projected, 'tp', scatter_dimension=0, tiled=True)  31.7 us
  transfers between devices with their start and end apart: 5, of which 5 were waited for; matrix products, arithmetic and copies ran while one was open for 7% of the time, Pallas kernels for 0%

profile of v1, /device:TPU:1, one launch (start us, length us, event | category | flops | bytes accessed | tf_op | source)
XLA Modules:
  0.0 1118.6 jit_solution(8841613759781395432)
XLA Ops:
  14.0 6.1 fusion.48
  43.7 15.2 %fusion.43 = s32[1024]{0:T(1024)S(1)} fusion(pred[1024]{0:T(1024)(128)(4,1)S(1)} %compare_reduce_fusion, pred[1024]{0:T(1024)(128)(4,1)S(1)} %compare_reduce_fusion.1, pred[1024]{0:T(1024)(128)(4,1)S(1)} %compare_reduce_fusion.2, pred[1024]{0:T(1024)(128)(4,1)S(1)} %compare_reduce_fusion.3, pred[1024]{0:T(1024)(128)(4,1)S(1)} %compare_reduce_fusion.4, ...), kind=kLoop, calls=%fused_computation.122 | loop fusion | flops 33792 | bytes 33892 | tf_op jit(solution)/shard_map/add | solution.py:59
  64.2 85.2 %all-gather.2.cloned.1.call-done = bf16[1024,2048]{1,0:T(8,128)(2,1)} async-done(((bf16[32,2048]{1,0:T(8,128)(2,1)}), bf16[1024,2048]{1,0:T(8,128)(2,1)}) %all-gather.2.cloned.1.call-update) | async-done | bytes 4194320 | tf_op jit(solution)/shard_map/all_gather | solution.py:56
  172.9 103.2 %while.37 = (s32[]{:T(128)}, f32[1024,8]{0,1:T(8,128)S(1)}, f32[1024,8]{0,1:T(8,128)S(1)}, f32[1024,8,128]{2,0,1:T(8,128)}, s32[]{:T(128)}, /*index=5*/bf16[24,1...) while((s32[]{:T(128)}, f32[1024,8]{0,1:T(8,128)S(1)}, ...), condition=%wide.region_8.10_spmd.clone, body=%wide.region_5.9_spmd.clone.sunk | while | flops 2196807680 | bytes 62130376 | solution.py:94
  182.4 6.3 fusion.93
  198.3 7.9 fusion.93
  215.8 7.9 fusion.93
  233.3 7.9 fusion.93
  250.7 7.9 fusion.93
  268.2 7.9 fusion.93
  281.4 93.2 %while.36 = (s32[]{:T(128)}, f32[1024,8]{0,1:T(8,128)S(1)}, f32[1024,8]{0,1:T(8,128)S(1)}, f32[1024,8,128]{2,0,1:T(8,128)}, s32[]{:T(128)}, /*index=5*/bf16[24,1...) while((s32[]{:T(128)}, f32[1024,8]{0,1:T(8,128)S(1)}, ...), condition=%wide.region_3.5_spmd.clone, body=%wide.region_0.4_spmd.clone.sunk | while | flops 2196807680 | bytes 62130376 | solution.py:94
  289.3 6.3 fusion.86
  303.6 7.9 fusion.86
  319.4 7.9 fusion.86
  335.2 7.9 fusion.86
  350.9 7.9 fusion.86
  366.7 7.9 fusion.86
  389.6 269.2 %all-reduce.2.cloned.1.call-done = f32[1024,16]{0,1:T(8,128)} async-done(((f32[1024,16]{0,1:T(8,128)}), f32[1024,16]{0,1:T(8,128)}) %all-reduce.2.cloned.1.call-update) | async-done | bytes 65552 | tf_op jit(solution)/shard_map/pmax | solution.py:109
  660.8 8.7 maximum_multiply_fusion
  669.4 9.1 copy.64
  678.7 130.2 %reduce-scatter.12.cloned.1.call-done = f32[32,16]{1,0:T(8,128)} async-done(((f32[1024,16]{1,0:T(8,128)}), f32[32,16]{1,0:T(8,128)}) %reduce-scatter.12.cloned.1.call-update) | async-done | bytes 2064
  809.7 209.7 %reduce-scatter.10.cloned.1.call-done = f32[32,2048]{1,0:T(8,128)} async-done(((f32[1024,2048]{1,0:T(8,128)}), f32[32,2048]{1,0:T(8,128)}) %reduce-scatter.10.cloned.1.call-update) | async-done | bytes 262160
  1021.5 56.6 %all_to_all.5 = bf16[32,32,2048]{2,1,0:T(8,128)(2,1)S(1)} all-to-all(bf16[32,32,2048]{2,1,0:T(8,128)(2,1)S(1)} %stack.2), channel_id=1, replica_groups=mesh['ctx'=32,'tp'=4] {'ctx'}, dimensions={0} | all-to-all | bytes 8388608 | tf_op jit(solution)/shard_map/all_to_all | solution.py:125
  1080.3 31.7 %reduce-scatter.8.cloned.1.call-done = f32[256,256]{1,0:T(8,128)} async-done(((f32[1024,256]{1,0:T(8,128)}), f32[256,256]{1,0:T(8,128)}) %reduce-scatter.8.cloned.1.call-update) | async-done | bytes 262160 | tf_op jit(solution)/shard_map/reduce_scatter | solution.py:130
  (210 shorter events, 191.0 us)
Async XLA Ops:
  6.5 1071.5 %copy-start = (bf16[2048,256]{1,0:T(8,128)(2,1)S(1)}, bf16[2048,256]{1,0:T(8,128)(2,1)}, u32[]{:S(2)}) copy-start(bf16[2048,256]{1,0:T(8,128)(2,1)} %param.23) | copy-start | bytes 3145732
  6.5 142.9 %all-gather.2.cloned.1.call-start = ((), (), s32[]{:S(2)}) async-start(), calls=%async_computation.4 | async-start | bytes 4325376 | tf_op jit(solution)/shard_map/all_gather | solution.py:56
  7.3 651.6 %all-reduce.2.cloned.1.call-start = ((), (), s32[]{:S(2)}) async-start(), calls=%async_computation.5 | async-start | bytes 131072 | tf_op jit(solution)/shard_map/pmax | solution.py:109
  7.4 6.6 copy-start.13
  28.5 4.2 copy-start.5
  28.5 7.3 copy-start.7
  28.5 14.5 %copy-start.12 = (s32[1,2]{1,0:T(1,128)S(1)}, s32[1,2]{1,0:T(1,128)}, u32[]{:S(2)}) copy-start(s32[1,2]{1,0:T(1,128)} %param.21) | copy-start | bytes 28
  34.3 27.5 %copy-start.6 = (bf16[24,128,128]{2,1,0:T(8,128)(2,1)S(1)}, bf16[24,128,128]{2,1,0:T(8,128)(2,1)}, u32[]{:S(2)}) copy-start(bf16[24,128,128]{2,1,0:T(8,128)(2,1)} %gather_fusion.1) | copy-start | bytes 2359300
  156.1 7.0 copy-start.10
  163.1 3.9 copy-start.1
  374.6 5.5 copy-start.9
  374.6 5.5 copy-start.4
  374.6 5.8 copy-start.8
  374.6 6.4 copy-start.3
  374.6 6.7 copy-start.11
  381.3 427.6 %reduce-scatter.12.cloned.1.call-start = ((), (), s32[]{:S(2)}) async-start(), calls=%async_computation.8 | async-start | bytes 540672
  381.4 5.5 copy-start.2
  660.7 358.6 %reduce-scatter.10.cloned.1.call-start = ((), (), s32[]{:S(2)}) async-start(), calls=%async_computation.7 | async-start | bytes 8650752
  678.6 433.4 %reduce-scatter.8.cloned.1.call-start = ((), (), s32[]{:S(2)}) async-start(), calls=%async_computation.6 | async-start | bytes 1310720 | tf_op jit(solution)/shard_map/reduce_scatter | solution.py:130
Sparse Core Ops, SparseCore 0:
  9.0 140.3 all-gather.1
  381.4 277.4 all-reduce.1
  661.3 147.4 reduce-scatter.11
  811.1 208.1 reduce-scatter.9
  1080.5 31.5 reduce-scatter.7
